TPU v7x, 32 devices: a whole 2x2x4 slice. The times are simulated.
32 devices in a mesh: grp: 2 (over y), seq: 4 (over z), sub: 4 (over x, core).
Axes of the slice: x: 2, y: 2, z: 4, core: 2. Of those that a mesh axis runs over, the one named last changes fastest.
Arguments:
- activations: bfloat16 [32768, 384], P(('grp', 'seq', 'sub')), parts along dimension 0, may hold values from -6 to 6
- cotangent: bfloat16 [32768, 384], P(('grp', 'seq', 'sub')), parts along dimension 0, may hold values from -6 to 6
- weights: bfloat16 [2304, 384], P('sub'), may hold values from -0.1875 to 0.1875
Outputs:
- input_grad: bfloat16 [32768, 384], P(('grp', 'seq', 'sub')), parts along dimension 0
- weight_grad: float32 [4608, 384], P(('grp', 'sub')), parts along dimension 0
There are 2 independent parts, one for each index of `grp`. A program takes and returns all parts, laid end to end along the dimension named above; an argument that names none is the same for every part. Nothing has to cross between parts.
All inputs are finite; a program needn't handle non-finite values.
Results may differ from a plain program's by a relative error of at most 0.0053.
Values may be sent and summed in bfloat16 or wider, within the bound.
No kernel may reach another device: no remote copies, remote signals or barrier semaphores. Data moves between devices by JAX's collectives and lax.ppermute only.
A program may use at most 64 MiB of HBM per device.

v0:
```python
import math
import jax
import jax.numpy as jnp
from jax import lax
from jax.sharding import PartitionSpec as P

DILATION_FIRST = 1024
DILATION_SECOND = 2048


def from_behind(block, axis, distance):
    devices = range(lax.axis_size(axis))
    route = [(i - distance, i) for i in devices if i - distance in devices]
    return lax.ppermute(block, axis, route)


def gelu_pair(pre_act):
    coeff = 0.7978845608
    tanh_value = jnp.tanh(coeff * (pre_act + 0.044715 * pre_act * pre_act * pre_act))
    gelu_value = 0.5 * pre_act * (1.0 + tanh_value)
    gelu_slope = 0.5 * (1.0 + tanh_value) + 0.5 * pre_act * (
        1.0 - tanh_value * tanh_value
    ) * coeff * (1.0 + 3.0 * 0.044715 * pre_act * pre_act)
    return (gelu_value, gelu_slope)


def back_product(spread, kernel, count_of_rows, channels):
    spread_three = spread.reshape(count_of_rows, 3, channels)
    kernel_three = kernel.reshape(3, channels, channels)
    return lax.dot_general(
        spread_three, kernel_three, (((1, 2), (0, 2)), ((), ())), preferred_element_type=jnp.float32
    )


def tap_grads(stacked, delta):
    return lax.dot_general(
        stacked, delta, (((0,), (0,)), ((), ())), preferred_element_type=jnp.float32
    )


def per_device(activations, cotangent, weights):
    count_of_rows, channels = activations.shape
    devices = lax.axis_size("seq") * lax.axis_size("sub")
    nearby_jumps = DILATION_FIRST // count_of_rows
    distant_jumps = DILATION_SECOND // count_of_rows
    grad_scale = 1.0 / math.sqrt(count_of_rows * devices)
    all_weights = lax.all_gather(weights, "sub", axis=0, tiled=True)
    first = all_weights[: 3 * channels]
    second = all_weights[3 * channels :]

    def near_rows(source, sign):
        return from_behind(source, ("seq", "sub"), sign * nearby_jumps)

    def far_rows(source, sign):
        return from_behind(source, ("seq", "sub"), sign * distant_jumps)

    first_layer_weights = jnp.concatenate(
        (near_rows(activations, 1), activations, near_rows(activations, -1)), 1
    )
    pre_one = jnp.dot(first_layer_weights, first, preferred_element_type=jnp.float32)
    gelu_one, slope_one = gelu_pair(pre_one)
    middle_state = (activations.astype(jnp.float32) + gelu_one).astype(jnp.bfloat16)
    second_layer_weights = jnp.concatenate(
        (far_rows(middle_state, 1), middle_state, far_rows(middle_state, -1)), 1
    )
    pre_two = jnp.dot(second_layer_weights, second, preferred_element_type=jnp.float32)
    gelu_two, slope_two = gelu_pair(pre_two)
    second_error = (cotangent.astype(jnp.float32) * slope_two).astype(jnp.bfloat16)
    grad_two = tap_grads(second_layer_weights, second_error) * grad_scale
    second_reach = jnp.concatenate(
        (far_rows(second_error, -1), second_error, far_rows(second_error, 1)), 1
    )
    back_one = cotangent.astype(jnp.float32) + back_product(
        second_reach, second, count_of_rows, channels
    )
    first_error = (back_one * slope_one).astype(jnp.bfloat16)
    grad_one = tap_grads(first_layer_weights, first_error) * grad_scale
    first_reach = jnp.concatenate(
        (near_rows(first_error, -1), first_error, near_rows(first_error, 1)), 1
    )
    input_grad = (back_one + back_product(first_reach, first, count_of_rows, channels)).astype(
        jnp.bfloat16
    )
    local_grads = jnp.concatenate((grad_one, grad_two), 0)
    summed = lax.psum(local_grads, "seq")
    weight_grad = lax.psum_scatter(summed, "sub", scatter_dimension=0, tiled=True)
    return (input_grad, weight_grad)


def solution(mesh):
    placed = (P(("grp", "seq", "sub"), None), P(("grp", "seq", "sub"), None), P("sub", None))
    return jax.shard_map(
        per_device,
        mesh=mesh,
        in_specs=placed,
        out_specs=(P(("grp", "seq", "sub"), None), P(("grp", "sub"), None)),
        check_vma=False,
    )
```

profile of v0, /device:TPU:0, one launch (start us, length us, event | category | flops | bytes accessed | tf_op | source)
XLA Modules:
  0.0 237.5 jit_solution(14820011768576403430)
XLA Ops:
  7.2 0.0 copy-start
  7.2 0.0 all-gather.2.cloned.1.call-start
  7.2 0.7 all-gather.2.cloned.1.call-update
  7.9 0.0 reduce-scatter.2.cloned.1.call-start
  8.0 2.4 %collective-permute-start = (bf16[1024,384]{1,0:T(8,128)(2,1)}, bf16[1024,384]{1,0:T(8,128)(2,1)S(1)}, u32[]{:S(2)}, u32[]{:S(2)}) collective-permute-start(bf16[1024,384]{1,0:T(8,128)(2,1)} %param.3), channel_id=1, source_target_pairs={{0,1},{1,2},{2,3},{3,4},{4,5},{5,6},{6,7},{7,8},{8,9},{9,10},{10,1... | collective-permute-start | bytes 2359304 | tf_op jit(solution)/shard_map/ppermute | solution.py:14
  10.4 1.3 collective-permute-start.1
  11.7 1.4 copy.6
  13.1 0.0 collective-permute-done
  13.1 1.0 constant_dynamic-update-slice_fusion.2
  14.1 0.0 copy-done
  14.1 1.0 constant_dynamic-update-slice_fusion.1
  15.1 1.7 collective-permute-done.1
  16.8 1.0 constant_dynamic-update-slice_fusion
  17.8 22.2 %all-gather.2.cloned.1.call-done = bf16[2304,384]{1,0:T(8,128)(2,1)} async-done(((bf16[576,384]{1,0:T(8,128)(2,1)}), bf16[2304,384]{1,0:T(8,128)(2,1)}) %all-gather.2.cloned.1.call-update) | async-done | bytes 1769488 | tf_op jit(solution)/shard_map/all_gather | solution.py:47
  40.0 4.9 %add_convert_fusion = (bf16[1024,384]{0,1:T(8,128)(2,1)}, f32[1024,384]{0,1:T(8,128)}) fusion(bf16[1024,384]{0,1:T(8,128)(2,1)S(1)} %copy.6, bf16[1024,1152]{1,0:T(8,128)(2,1)} %constant_dynamic-update-slice_fusion, bf16[2304,384]{1,0:T(8,128)(2,1)} %all-gather.2.cloned.1.call-done), kind=kOutput, calls=%fused_computation.27 | convolution fusion | flops 910295040 | bytes 6389760 | tf_op jit(solution)/shard_map/dot_general | solution.py:60
  44.9 1.3 collective-permute-start.3
  46.2 7.3 %collective-permute-start.2 = (bf16[1024,384]{0,1:T(8,128)(2,1)}, bf16[1024,384]{0,1:T(8,128)(2,1)}, u32[]{:S(2)}, u32[]{:S(2)}) collective-permute-start(bf16[1024,384]{0,1:T(8,128)(2,1)} %get-tuple-element.6), channel_id=1, source_target_pairs={{0,2},{1,3},{2,4},{3,5},{4,6},{5,7},{6,8},{7,9},{8,10},{9,11},{10,... | collective-permute-start | bytes 2359304 | tf_op jit(solution)/shard_map/ppermute | solution.py:14
  53.5 0.0 copy-done.2
  53.5 0.3 copy.5
  53.8 15.1 %collective-permute-done.3 = bf16[1024,384]{0,1:T(8,128)(2,1)} collective-permute-done((bf16[1024,384]{0,1:T(8,128)(2,1)}, bf16[1024,384]{0,1:T(8,128)(2,1)}, u32[]{:S(2)}, u32[]{:S(2)}) %collective-permute-start.3) | collective-permute-done | bytes 786464 | tf_op jit(solution)/shard_map/ppermute | solution.py:14
  68.9 17.0 %collective-permute-done.2 = bf16[1024,384]{0,1:T(8,128)(2,1)} collective-permute-done((bf16[1024,384]{0,1:T(8,128)(2,1)}, bf16[1024,384]{0,1:T(8,128)(2,1)}, u32[]{:S(2)}, u32[]{:S(2)}) %collective-permute-start.2) | collective-permute-done | bytes 786464 | tf_op jit(solution)/shard_map/ppermute | solution.py:14
  85.9 0.0 copy-done.1
  85.9 3.7 %fusion = bf16[1024,384]{0,1:T(8,128)(2,1)S(1)} fusion(bf16[1024,384]{0,1:T(8,128)(2,1)S(1)} %copy.5, bf16[1024,384]{0,1:T(8,128)(2,1)} %collective-permute-done.3, bf16[1024,384]{0,1:T(8,128)(2,1)} %get-tuple-element.6, bf16[1024,384]{0,1:T(8,128)(2,1)} %collective-permute-done.2, bf16[2304,384]{1,0:T(8,128)(2,1)S(1)} %copy-done.1), kind=kOutput, calls=%fused_computation.12 | convolution fusion | flops 920911872 | bytes 4816896 | tf_op jit(solution)/shard_map/dot_general | solution.py:66
  89.6 4.4 %collective-permute-start.5 = (bf16[1024,384]{0,1:T(8,128)(2,1)S(1)}, bf16[1024,384]{0,1:T(8,128)(2,1)S(1)}, u32[]{:S(2)}, u32[]{:S(2)}) collective-permute-start(bf16[1024,384]{0,1:T(8,128)(2,1)S(1)} %fusion), channel_id=1, source_target_pairs={{0,2},{1,3},{2,4},{3,5},{4,6},{5,7},{6,8},{7,9},{8,10},{9,11},{10,... | collective-permute-start | bytes 2359304 | tf_op jit(solution)/shard_map/ppermute | solution.py:14
  94.0 1.3 collective-permute-start.4
  95.3 0.2 fusion.20
  95.5 3.0 %convolution_multiply_fusion = f32[1152,384]{1,0:T(8,128)S(1)} fusion(bf16[1024,384]{0,1:T(8,128)(2,1)S(1)} %fusion, bf16[1024,384]{0,1:T(8,128)(2,1)} %collective-permute-done.3, bf16[1024,384]{0,1:T(8,128)(2,1)} %get-tuple-element.6, bf16[1024,384]{0,1:T(8,128)(2,1)} %collective-permute-done.2), kind=kOutput, calls=%fused_computation.1 | convolution fusion | flops 913489920 | bytes 4915200 | tf_op jit(solution)/shard_map/dot_general | solution.py:36
  98.6 0.0 copy-start.4
  98.6 29.3 %collective-permute-done.5 = bf16[1024,384]{0,1:T(8,128)(2,1)S(1)} collective-permute-done((bf16[1024,384]{0,1:T(8,128)(2,1)S(1)}, bf16[1024,384]{0,1:T(8,128)(2,1)S(1)}, u32[]{:S(2)}, u32[]{:S(2)}) %collective-permute-start.5) | collective-permute-done | bytes 786464 | tf_op jit(solution)/shard_map/ppermute | solution.py:14
  127.8 0.0 collective-permute-done.4
  127.8 0.2 pad_maximum_fusion.2
  128.1 3.0 %fusion.12 = (bf16[1024,384]{0,1:T(8,128)(2,1)S(1)}, f32[1024,384]{0,1:T(8,128)}) fusion(f32[1024,384]{0,1:T(8,128)S(1)} %copy-done.4, bf16[3,384,384]{2,1,0:T(8,128)(2,1)S(1)} %bitcast.21, bf16[1024,3,384]{0,2,1:T(8,128)(2,1)S(1)} %bitcast.18, bf16[1024,384]{0,1:T(8,128)(2,1)S(1)} %copy.5), kind=kOutput, calls=%fused_computation.24 | convolution fusion | flops 914227200 | bytes 7962624 | tf_op jit(solution)/shard_map/dot_general | solution.py:30
  131.1 3.1 %convolution_multiply_fusion.1 = f32[1152,384]{1,0:T(8,128)S(1)} fusion(bf16[1024,1152]{1,0:T(8,128)(2,1)} %constant_dynamic-update-slice_fusion, bf16[1024,384]{0,1:T(8,128)(2,1)S(1)} %get-tuple-element.8), kind=kOutput, calls=%fused_computation.2 | convolution fusion | flops 906412032 | bytes 4915200 | tf_op jit(solution)/shard_map/dot_general | solution.py:36
  134.2 2.0 pad_maximum_fusion
  136.2 0.0 reduce-scatter.2.cloned.1.call-update
  136.2 0.0 all-reduce.2.cloned.1.call-start
  136.3 1.3 collective-permute-start.7
  137.6 1.3 collective-permute-start.6
  138.9 39.1 %reduce-scatter.2.cloned.1.call-done = f32[576,384]{1,0:T(8,128)} async-done(((f32[2304,384]{1,0:T(8,128)}), f32[576,384]{1,0:T(8,128)}) %reduce-scatter.2.cloned.1.call-update) | async-done | bytes 884752 | tf_op jit(solution)/shard_map/reduce_scatter | solution.py:86
  178.0 0.0 all-reduce.2.cloned.1.call-update
  178.1 0.0 collective-permute-done.7
  178.1 0.0 collective-permute-done.6
  178.1 0.2 pad_maximum_fusion.3
  178.3 1.2 copy-done.3
  179.5 1.2 fusion.13
  180.7 1.2 copy.10
  181.8 47.0 %all-reduce.2.cloned.1.call-done = f32[576,384]{1,0:T(8,128)} async-done(((f32[576,384]{1,0:T(8,128)}), f32[576,384]{1,0:T(8,128)}) %all-reduce.2.cloned.1.call-update) | async-done | bytes 884752 | tf_op jit(solution)/shard_map/psum | solution.py:85
  228.8 2.1 copy.18
  (4 shorter events, 0.0 us)
Async XLA Ops:
  7.2 6.9 %copy-start = (bf16[1024,384]{1,0:T(8,128)(2,1)S(1)}, bf16[1024,384]{1,0:T(8,128)(2,1)}, u32[]{:S(2)}) copy-start(bf16[1024,384]{1,0:T(8,128)(2,1)} %param.3) | copy-start | bytes 2359300
  7.2 32.8 %all-gather.2.cloned.1.call-start = ((), (), s32[]{:S(2)}) async-start(), calls=%async_computation.1 | async-start | bytes 2211840 | tf_op jit(solution)/shard_map/all_gather | solution.py:47
  7.9 170.1 %reduce-scatter.2.cloned.1.call-start = ((), (), s32[]{:S(2)}) async-start(), calls=%async_computation.2 | async-start | bytes 4423680 | tf_op jit(solution)/shard_map/reduce_scatter | solution.py:86
  8.0 5.1 %collective-permute-start = (bf16[1024,384]{1,0:T(8,128)(2,1)}, bf16[1024,384]{1,0:T(8,128)(2,1)S(1)}, u32[]{:S(2)}, u32[]{:S(2)}) collective-permute-start(bf16[1024,384]{1,0:T(8,128)(2,1)} %param.3), channel_id=1, source_target_pairs={{0,1},{1,2},{2,3},{3,4},{4,5},{5,6},{6,7},{7,8},{8,9},{9,10},{10,1... | collective-permute-start | bytes 2359304 | tf_op jit(solution)/shard_map/ppermute | solution.py:14
  10.4 6.4 %collective-permute-start.1 = (bf16[1024,384]{1,0:T(8,128)(2,1)}, bf16[1024,384]{1,0:T(8,128)(2,1)S(1)}, u32[]{:S(2)}, u32[]{:S(2)}) collective-permute-start(bf16[1024,384]{1,0:T(8,128)(2,1)} %param.3), channel_id=1, source_target_pairs={{1,0},{2,1},{3,2},{4,3},{5,4},{6,5},{7,6},{8,7},{9,8},{10,9},{11,1... | collective-permute-start | bytes 2359304 | tf_op jit(solution)/shard_map/ppermute | solution.py:14
  17.8 35.7 %copy-start.2 = (bf16[1024,384]{1,0:T(8,128)(2,1)S(1)}, bf16[1024,384]{1,0:T(8,128)(2,1)}, u32[]{:S(2)}) copy-start(bf16[1024,384]{1,0:T(8,128)(2,1)} %param.4) | copy-start | bytes 2359300
  40.0 46.0 %copy-start.1 = (bf16[2304,384]{1,0:T(8,128)(2,1)S(1)}, bf16[2304,384]{1,0:T(8,128)(2,1)}, u32[]{:S(2)}) copy-start(bf16[2304,384]{1,0:T(8,128)(2,1)} %all-gather.2.cloned.1.call-done) | copy-start | bytes 5308420
  44.9 24.0 %collective-permute-start.3 = (bf16[1024,384]{0,1:T(8,128)(2,1)}, bf16[1024,384]{0,1:T(8,128)(2,1)}, u32[]{:S(2)}, u32[]{:S(2)}) collective-permute-start(bf16[1024,384]{0,1:T(8,128)(2,1)} %get-tuple-element.6), channel_id=1, source_target_pairs={{2,0},{3,1},{4,2},{5,3},{6,4},{7,5},{8,6},{9,7},{10,8},{11,9},{12,... | collective-permute-start | bytes 2359304 | tf_op jit(solution)/shard_map/ppermute | solution.py:14
  46.2 39.7 %collective-permute-start.2 = (bf16[1024,384]{0,1:T(8,128)(2,1)}, bf16[1024,384]{0,1:T(8,128)(2,1)}, u32[]{:S(2)}, u32[]{:S(2)}) collective-permute-start(bf16[1024,384]{0,1:T(8,128)(2,1)} %get-tuple-element.6), channel_id=1, source_target_pairs={{0,2},{1,3},{2,4},{3,5},{4,6},{5,7},{6,8},{7,9},{8,10},{9,11},{10,... | collective-permute-start | bytes 2359304 | tf_op jit(solution)/shard_map/ppermute | solution.py:14
  89.6 38.2 %collective-permute-start.5 = (bf16[1024,384]{0,1:T(8,128)(2,1)S(1)}, bf16[1024,384]{0,1:T(8,128)(2,1)S(1)}, u32[]{:S(2)}, u32[]{:S(2)}) collective-permute-start(bf16[1024,384]{0,1:T(8,128)(2,1)S(1)} %fusion), channel_id=1, source_target_pairs={{0,2},{1,3},{2,4},{3,5},{4,6},{5,7},{6,8},{7,9},{8,10},{9,11},{10,... | collective-permute-start | bytes 2359304 | tf_op jit(solution)/shard_map/ppermute | solution.py:14
  94.0 33.8 %collective-permute-start.4 = (bf16[1024,384]{0,1:T(8,128)(2,1)S(1)}, bf16[1024,384]{0,1:T(8,128)(2,1)S(1)}, u32[]{:S(2)}, u32[]{:S(2)}) collective-permute-start(bf16[1024,384]{0,1:T(8,128)(2,1)S(1)} %fusion), channel_id=1, source_target_pairs={{2,0},{3,1},{4,2},{5,3},{6,4},{7,5},{8,6},{9,7},{10,8},{11,9},{12,... | collective-permute-start | bytes 2359304 | tf_op jit(solution)/shard_map/ppermute | solution.py:14
  98.6 29.5 %copy-start.4 = (f32[1024,384]{0,1:T(8,128)S(1)}, f32[1024,384]{0,1:T(8,128)}, u32[]{:S(2)}) copy-start(f32[1024,384]{0,1:T(8,128)} %get-tuple-element.7) | copy-start | bytes 4718596
  136.2 92.6 %all-reduce.2.cloned.1.call-start = ((), (), s32[]{:S(2)}) async-start(), calls=%async_computation.3 | async-start | bytes 1769472 | tf_op jit(solution)/shard_map/psum | solution.py:85
  136.3 41.8 %collective-permute-start.7 = (bf16[1024,384]{0,1:T(8,128)(2,1)S(1)}, bf16[1024,384]{0,1:T(8,128)(2,1)S(1)}, u32[]{:S(2)}, u32[]{:S(2)}) collective-permute-start(bf16[1024,384]{0,1:T(8,128)(2,1)S(1)} %get-tuple-element.8), channel_id=1, source_target_pairs={{0,1},{1,2},{2,3},{3,4},{4,5},{5,6},{6,7},{7,8},{8,9},{9,10},{10,1... | collective-permute-start | bytes 2359304 | tf_op jit(solution)/shard_map/ppermute | solution.py:14
  137.6 40.5 %collective-permute-start.6 = (bf16[1024,384]{0,1:T(8,128)(2,1)S(1)}, bf16[1024,384]{0,1:T(8,128)(2,1)S(1)}, u32[]{:S(2)}, u32[]{:S(2)}) collective-permute-start(bf16[1024,384]{0,1:T(8,128)(2,1)S(1)} %get-tuple-element.8), channel_id=1, source_target_pairs={{1,0},{2,1},{3,2},{4,3},{5,4},{6,5},{7,6},{8,7},{9,8},{10,9},{11,1... | collective-permute-start | bytes 2359304 | tf_op jit(solution)/shard_map/ppermute | solution.py:14
  178.1 1.4 copy-start.3
Sparse Core Ops, SparseCore 0:
  9.6 30.3 all-gather.1
  136.3 41.6 reduce-scatter.1
  180.5 48.2 all-reduce.1
where the time goes:
time: 238 us; the launch traced here: 237 us
  waiting for transfers between devices  172 us (72%)
  starting transfers between devices  20.8 us (9%)
  matrix products  18.9 us (8%)
  between operations  13.9 us (6%)
  local copies, waits for them, and re-layouts  9.33 us (4%)
  other arithmetic  2.4 us (1%)
    ppermute x8, waiting for transfers between devices, from_behind(): return lax.ppermute(block, axis, route)  63.1 us
    psum x1, waiting for transfers between devices, per_device(): summed = lax.psum(local_grads, 'seq')  47 us
    reduce_scatter x1, waiting for transfers between devices, per_device(): lax.psum_scatter(summed, 'sub', scatter_dimension=0, tiled=True)  39.1 us
    all_gather x1, waiting for transfers between devices, per_device(): all_weights = lax.all_gather(weights, 'sub', axis=0, tiled=True)  22.2 us
    ppermute x8, starting transfers between devices, from_behind(): return lax.ppermute(block, axis, route)  20.7 us
    unnamed x16, local copies, waits for them, and re-layouts  8.17 us
    dot_general x2, matrix products, tap_grads(): lax.dot_general(stacked, delta, (((0,), (0,)), ((), ())), preferred_eleme...  6.12 us
    dot_general x1, matrix products, per_device(): jnp.dot(first_layer_weights, first, preferred_element_type=jnp.float32)  4.94 us
  transfers between devices with their start and end apart: 11, of which 7 were waited for; matrix products, arithmetic and copies ran while one was open for 4% of the time, Pallas kernels for 0%

commit v1 on v0

--- a/solution.py
+++ b/solution.py
@@ -44,7 +44,17 @@
     nearby_jumps = DILATION_FIRST // count_of_rows
     distant_jumps = DILATION_SECOND // count_of_rows
     grad_scale = 1.0 / math.sqrt(count_of_rows * devices)
-    all_weights = lax.all_gather(weights, "sub", axis=0, tiled=True)
+    size_here = lax.axis_size("sub")
+    arr_now = weights
+    found_now = [(b - 1, b) for b in range(1, size_here)] + [(size_here - 1, 0)]
+    h = 0
+    by_rank = [arr_now]
+    while h < size_here - 1:
+        arr_now = lax.ppermute(arr_now, axis_name="sub", perm=found_now)
+        by_rank += [arr_now]
+        h += 1
+    left_arr = jnp.concatenate([*reversed(by_rank)], axis=0)
+    all_weights = jnp.roll(left_arr, shift=(lax.axis_index("sub") + 1) * arr_now.shape[0], axis=0)
     first = all_weights[: 3 * channels]
     second = all_weights[3 * channels :]
 

time: 238 us -> 238 us (level)
  starting transfers between devices: 20.8 us -> 35 us
  waiting for transfers between devices: 172 us -> 159 us
  matrix products: 18.9 us -> 15.3 us
    all_gather x1 -> x0, waiting for transfers between devices: 22.2 us -> none  [per_device(): all_weights = lax.all_gather(weights, 'sub', axis=0, tiled=True)]
    ppermute x0 -> x3, waiting for transfers between devices: none -> 13.9 us  [per_device(): arr_now = lax.ppermute(arr_now, axis_name='sub', perm=found_now)]
    ppermute x0 -> x3, starting transfers between devices: none -> 9.58 us  [per_device(): arr_now = lax.ppermute(arr_now, axis_name='sub', perm=found_now)]
    ppermute x8, starting transfers between devices: 20.7 us -> 25.4 us  [from_behind(): return lax.ppermute(block, axis, route)]
    ppermute x8, waiting for transfers between devices: 63.1 us -> 59.4 us  [from_behind(): return lax.ppermute(block, axis, route)]
    unnamed x16 -> x29, local copies, waits for them, and re-layouts: 8.17 us -> 10.1 us
  transfers between devices with their start and end apart: 11 -> 13, of which waited for: 7 -> 7; matrix products, arithmetic and copies ran while one was open for 4% -> 4% of each run, Pallas kernels for 0% -> 0%
where the time goes in v1:
time: 238 us; the launch traced here: 237 us
  waiting for transfers between devices  159 us (67%)
  starting transfers between devices  35 us (15%)
  matrix products  15.3 us (6%)
  between operations  14.3 us (6%)
  local copies, waits for them, and re-layouts  10.8 us (5%)
  other arithmetic  2.4 us (1%)
    ppermute x8, waiting for transfers between devices, from_behind(): return lax.ppermute(block, axis, route)  59.4 us
    psum x1, waiting for transfers between devices, per_device(): summed = lax.psum(local_grads, 'seq')  47 us
    reduce_scatter x1, waiting for transfers between devices, per_device(): lax.psum_scatter(summed, 'sub', scatter_dimension=0, tiled=True)  39.2 us
    ppermute x8, starting transfers between devices, from_behind(): return lax.ppermute(block, axis, route)  25.4 us
    ppermute x3, waiting for transfers between devices, per_device(): arr_now = lax.ppermute(arr_now, axis_name='sub', perm=found_now)  13.9 us
    unnamed x29, local copies, waits for them, and re-layouts  10.1 us
    ppermute x3, starting transfers between devices, per_device(): arr_now = lax.ppermute(arr_now, axis_name='sub', perm=found_now)  9.58 us
  transfers between devices with their start and end apart: 13, of which 7 were waited for; matrix products, arithmetic and copies ran while one was open for 4% of the time, Pallas kernels for 0%

profile of v1, /device:TPU:0, one launch (start us, length us, event | category | flops | bytes accessed | tf_op | source)
XLA Modules:
  0.0 237.4 jit_solution(10314840016827278539)
XLA Ops:
  7.2 0.0 reduce-scatter.2.cloned.1.call-start
  7.2 0.5 collective-permute-start.2
  7.7 5.4 %collective-permute-start = (bf16[1024,384]{1,0:T(8,128)(2,1)}, bf16[1024,384]{1,0:T(8,128)(2,1)}, u32[]{:S(2)}, u32[]{:S(2)}) collective-permute-start(bf16[1024,384]{1,0:T(8,128)(2,1)} %param.3), channel_id=1, source_target_pairs={{0,1},{1,2},{2,3},{3,4},{4,5},{5,6},{6,7},{7,8},{8,9},{9,10},{10,1... | collective-permute-start | bytes 2359304 | tf_op jit(solution)/shard_map/ppermute | solution.py:14
  13.1 1.3 collective-permute-start.1
  14.4 1.4 collective-permute-done.2
  15.8 0.0 collective-permute-start.3
  15.9 12.4 %collective-permute-done.3 = bf16[576,384]{1,0:T(8,128)(2,1)S(1)} collective-permute-done((bf16[576,384]{1,0:T(8,128)(2,1)S(1)}, bf16[576,384]{1,0:T(8,128)(2,1)S(1)}, u32[]{:S(2)}, u32[]{:S(2)}) %collective-permute-start.3) | collective-permute-done | bytes 442400 | tf_op jit(solution)/shard_map/ppermute | solution.py:53
  28.3 9.0 %collective-permute-start.4 = (bf16[576,384]{1,0:T(8,128)(2,1)S(1)}, bf16[576,384]{1,0:T(8,128)(2,1)S(1)}, u32[]{:S(2)}, u32[]{:S(2)}) collective-permute-start(bf16[576,384]{1,0:T(8,128)(2,1)S(1)} %collective-permute-done.3), channel_id=1, source_target_pairs={{0,1},{1,2},{2,3},{3,0},{4,5},{5,6},{6,7},{7,4},{8,9},{9,10},{10,1... | collective-permute-start | bytes 1327112 | tf_op jit(solution)/shard_map/ppermute | solution.py:53
  37.4 2.3 copy.6
  39.7 1.2 constant_dynamic-update-slice_fusion.10
  40.9 0.2 constant_dynamic-update-slice_fusion.9
  41.1 0.2 constant_dynamic-update-slice_fusion.8
  41.3 0.1 constant_dynamic-update-slice_fusion.6
  41.4 0.1 constant_dynamic-update-slice_fusion.5
  41.5 0.6 copy-done.1
  42.1 0.1 constant_dynamic-update-slice_fusion.4
  42.1 0.1 constant_dynamic-update-slice_fusion.3
  42.2 0.1 constant_dynamic-update-slice_fusion.2
  42.3 0.1 constant_dynamic-update-slice_fusion.1
  42.4 0.1 constant_dynamic-update-slice_fusion
  42.5 0.5 constant_dynamic-slice_fusion.1
  43.0 0.6 copy-done.3
  43.5 3.0 %add_convert_fusion = (bf16[1024,384]{0,1:T(8,128)(2,1)}, f32[1024,384]{0,1:T(8,128)}) fusion(bf16[1024,384]{0,1:T(8,128)(2,1)S(1)} %copy-done.3, bf16[1024,1152]{1,0:T(8,128)(2,1)S(1)} %constant_dynamic-update-slice_fusion.8, bf16[1152,384]{1,0:T(8,128)(2,1)S(1)} %get-tuple-element.4), kind=kOutput, calls=%fused_computation.27 | convolution fusion | flops 910295040 | bytes 6389760 | tf_op jit(solution)/shard_map/dot_general | solution.py:70
  46.5 1.3 collective-permute-start.6
  47.8 9.1 %collective-permute-start.5 = (bf16[1024,384]{0,1:T(8,128)(2,1)}, bf16[1024,384]{0,1:T(8,128)(2,1)}, u32[]{:S(2)}, u32[]{:S(2)}) collective-permute-start(bf16[1024,384]{0,1:T(8,128)(2,1)} %get-tuple-element.6), channel_id=1, source_target_pairs={{0,2},{1,3},{2,4},{3,5},{4,6},{5,7},{6,8},{7,9},{8,10},{9,11},{10,... | collective-permute-start | bytes 2359304 | tf_op jit(solution)/shard_map/ppermute | solution.py:14
  56.8 0.3 copy.5
  57.1 14.3 %collective-permute-done.6 = bf16[1024,384]{0,1:T(8,128)(2,1)} collective-permute-done((bf16[1024,384]{0,1:T(8,128)(2,1)}, bf16[1024,384]{0,1:T(8,128)(2,1)}, u32[]{:S(2)}, u32[]{:S(2)}) %collective-permute-start.6) | collective-permute-done | bytes 786464 | tf_op jit(solution)/shard_map/ppermute | solution.py:14
  71.4 15.7 %collective-permute-done.5 = bf16[1024,384]{0,1:T(8,128)(2,1)} collective-permute-done((bf16[1024,384]{0,1:T(8,128)(2,1)}, bf16[1024,384]{0,1:T(8,128)(2,1)}, u32[]{:S(2)}, u32[]{:S(2)}) %collective-permute-start.5) | collective-permute-done | bytes 786464 | tf_op jit(solution)/shard_map/ppermute | solution.py:14
  87.1 3.7 %fusion = bf16[1024,384]{0,1:T(8,128)(2,1)S(1)} fusion(bf16[1024,384]{0,1:T(8,128)(2,1)S(1)} %copy.5, bf16[1152,384]{1,0:T(8,128)(2,1)S(1)} %get-tuple-element.5, bf16[1024,384]{0,1:T(8,128)(2,1)} %collective-permute-done.6, bf16[1024,384]{0,1:T(8,128)(2,1)} %get-tuple-element.6, bf16[1024,384]{0,1:T(8,128)(2,1)} %collective-permute-done.5), kind=kOutput, calls=%fused_computation.12 | convolution fusion | flops 920911872 | bytes 4816896 | tf_op jit(solution)/shard_map/dot_general | solution.py:76
  90.7 4.4 %collective-permute-start.8 = (bf16[1024,384]{0,1:T(8,128)(2,1)S(1)}, bf16[1024,384]{0,1:T(8,128)(2,1)S(1)}, u32[]{:S(2)}, u32[]{:S(2)}) collective-permute-start(bf16[1024,384]{0,1:T(8,128)(2,1)S(1)} %fusion), channel_id=1, source_target_pairs={{0,2},{1,3},{2,4},{3,5},{4,6},{5,7},{6,8},{7,9},{8,10},{9,11},{10,... | collective-permute-start | bytes 2359304 | tf_op jit(solution)/shard_map/ppermute | solution.py:14
  95.2 1.3 collective-permute-start.7
  96.5 3.0 %convolution_multiply_fusion = f32[1152,384]{1,0:T(8,128)S(1)} fusion(bf16[1024,384]{0,1:T(8,128)(2,1)S(1)} %fusion, bf16[1024,384]{0,1:T(8,128)(2,1)} %collective-permute-done.6, bf16[1024,384]{0,1:T(8,128)(2,1)} %get-tuple-element.6, bf16[1024,384]{0,1:T(8,128)(2,1)} %collective-permute-done.5), kind=kOutput, calls=%fused_computation.1 | convolution fusion | flops 913489920 | bytes 4915200 | tf_op jit(solution)/shard_map/dot_general | solution.py:36
  99.5 29.4 %collective-permute-done.8 = bf16[1024,384]{0,1:T(8,128)(2,1)S(1)} collective-permute-done((bf16[1024,384]{0,1:T(8,128)(2,1)S(1)}, bf16[1024,384]{0,1:T(8,128)(2,1)S(1)}, u32[]{:S(2)}, u32[]{:S(2)}) %collective-permute-start.8) | collective-permute-done | bytes 786464 | tf_op jit(solution)/shard_map/ppermute | solution.py:14
  129.0 0.2 pad_maximum_fusion.2
  129.2 3.1 %fusion.12 = (bf16[1024,384]{0,1:T(8,128)(2,1)S(1)}, f32[1024,384]{0,1:T(8,128)}) fusion(f32[1024,384]{0,1:T(8,128)S(1)} %copy-done.7, bf16[3,384,384]{2,1,0:T(8,128)(2,1)S(1)} %bitcast.23, bf16[1024,3,384]{0,2,1:T(8,128)(2,1)S(1)} %bitcast.20, bf16[1024,384]{0,1:T(8,128)(2,1)S(1)} %copy.5), kind=kOutput, calls=%fused_computation.24 | convolution fusion | flops 914227200 | bytes 7962624 | tf_op jit(solution)/shard_map/dot_general | solution.py:30
  132.3 1.4 convolution_multiply_fusion.1
  133.7 2.0 pad_maximum_fusion
  135.7 0.0 reduce-scatter.2.cloned.1.call-update
  135.7 0.0 all-reduce.2.cloned.1.call-start
  135.8 1.3 collective-permute-start.10
  137.1 1.3 collective-permute-start.9
  138.4 39.2 %reduce-scatter.2.cloned.1.call-done = f32[576,384]{1,0:T(8,128)} async-done(((f32[2304,384]{1,0:T(8,128)}), f32[576,384]{1,0:T(8,128)}) %reduce-scatter.2.cloned.1.call-update) | async-done | bytes 884752 | tf_op jit(solution)/shard_map/reduce_scatter | solution.py:96
  177.7 0.2 pad_maximum_fusion.3
  177.9 1.2 copy-done.6
  179.1 1.2 fusion.13
  180.2 1.2 copy.10
  181.4 47.0 %all-reduce.2.cloned.1.call-done = f32[576,384]{1,0:T(8,128)} async-done(((f32[576,384]{1,0:T(8,128)}), f32[576,384]{1,0:T(8,128)}) %all-reduce.2.cloned.1.call-update) | async-done | bytes 884752 | tf_op jit(solution)/shard_map/psum | solution.py:95
  228.4 2.1 copy.25
  (21 shorter events, 0.1 us)
Async XLA Ops:
  7.2 33.7 %copy-start = (bf16[1024,384]{1,0:T(8,128)(2,1)S(1)}, bf16[1024,384]{1,0:T(8,128)(2,1)}, u32[]{:S(2)}) copy-start(bf16[1024,384]{1,0:T(8,128)(2,1)} %param.3) | copy-start | bytes 2359300
  7.2 170.4 %reduce-scatter.2.cloned.1.call-start = ((), (), s32[]{:S(2)}) async-start(), calls=%async_computation.1 | async-start | bytes 4423680 | tf_op jit(solution)/shard_map/reduce_scatter | solution.py:96
  7.2 8.6 %collective-permute-start.2 = (bf16[576,384]{1,0:T(8,128)(2,1)}, bf16[576,384]{1,0:T(8,128)(2,1)S(1)}, u32[]{:S(2)}, u32[]{:S(2)}) collective-permute-start(bf16[576,384]{1,0:T(8,128)(2,1)} %param.5), channel_id=1, source_target_pairs={{0,1},{1,2},{2,3},{3,0},{4,5},{5,6},{6,7},{7,4},{8,9},{9,10},{10,1... | collective-permute-start | bytes 1327112 | tf_op jit(solution)/shard_map/ppermute | solution.py:53
  7.7 31.9 %collective-permute-start = (bf16[1024,384]{1,0:T(8,128)(2,1)}, bf16[1024,384]{1,0:T(8,128)(2,1)}, u32[]{:S(2)}, u32[]{:S(2)}) collective-permute-start(bf16[1024,384]{1,0:T(8,128)(2,1)} %param.3), channel_id=1, source_target_pairs={{0,1},{1,2},{2,3},{3,4},{4,5},{5,6},{6,7},{7,8},{8,9},{9,10},{10,1... | collective-permute-start | bytes 2359304 | tf_op jit(solution)/shard_map/ppermute | solution.py:14
  13.1 28.0 %collective-permute-start.1 = (bf16[1024,384]{1,0:T(8,128)(2,1)}, bf16[1024,384]{1,0:T(8,128)(2,1)S(1)}, u32[]{:S(2)}, u32[]{:S(2)}) collective-permute-start(bf16[1024,384]{1,0:T(8,128)(2,1)} %param.3), channel_id=1, source_target_pairs={{1,0},{2,1},{3,2},{4,3},{5,4},{6,5},{7,6},{8,7},{9,8},{10,9},{11,1... | collective-permute-start | bytes 2359304 | tf_op jit(solution)/shard_map/ppermute | solution.py:14
  15.8 12.5 %collective-permute-start.3 = (bf16[576,384]{1,0:T(8,128)(2,1)S(1)}, bf16[576,384]{1,0:T(8,128)(2,1)S(1)}, u32[]{:S(2)}, u32[]{:S(2)}) collective-permute-start(bf16[576,384]{1,0:T(8,128)(2,1)S(1)} %collective-permute-done.2), channel_id=1, source_target_pairs={{0,1},{1,2},{2,3},{3,0},{4,5},{5,6},{6,7},{7,4},{8,9},{9,10},{10,1... | collective-permute-start | bytes 1327112 | tf_op jit(solution)/shard_map/ppermute | solution.py:53
  28.3 12.9 %collective-permute-start.4 = (bf16[576,384]{1,0:T(8,128)(2,1)S(1)}, bf16[576,384]{1,0:T(8,128)(2,1)S(1)}, u32[]{:S(2)}, u32[]{:S(2)}) collective-permute-start(bf16[576,384]{1,0:T(8,128)(2,1)S(1)} %collective-permute-done.3), channel_id=1, source_target_pairs={{0,1},{1,2},{2,3},{3,0},{4,5},{5,6},{6,7},{7,4},{8,9},{9,10},{10,1... | collective-permute-start | bytes 1327112 | tf_op jit(solution)/shard_map/ppermute | solution.py:53
  41.1 1.0 copy-start.1
  41.2 1.7 copy-start.4
  42.4 1.1 copy-start.3
  43.5 13.3 %copy-start.2 = (bf16[1024,384]{1,0:T(8,128)(2,1)S(1)}, bf16[1024,384]{1,0:T(8,128)(2,1)}, u32[]{:S(2)}) copy-start(bf16[1024,384]{1,0:T(8,128)(2,1)} %param.4) | copy-start | bytes 2359300
  46.5 24.9 %collective-permute-start.6 = (bf16[1024,384]{0,1:T(8,128)(2,1)}, bf16[1024,384]{0,1:T(8,128)(2,1)}, u32[]{:S(2)}, u32[]{:S(2)}) collective-permute-start(bf16[1024,384]{0,1:T(8,128)(2,1)} %get-tuple-element.6), channel_id=1, source_target_pairs={{2,0},{3,1},{4,2},{5,3},{6,4},{7,5},{8,6},{9,7},{10,8},{11,9},{12,... | collective-permute-start | bytes 2359304 | tf_op jit(solution)/shard_map/ppermute | solution.py:14
  47.8 39.3 %collective-permute-start.5 = (bf16[1024,384]{0,1:T(8,128)(2,1)}, bf16[1024,384]{0,1:T(8,128)(2,1)}, u32[]{:S(2)}, u32[]{:S(2)}) collective-permute-start(bf16[1024,384]{0,1:T(8,128)(2,1)} %get-tuple-element.6), channel_id=1, source_target_pairs={{0,2},{1,3},{2,4},{3,5},{4,6},{5,7},{6,8},{7,9},{8,10},{9,11},{10,... | collective-permute-start | bytes 2359304 | tf_op jit(solution)/shard_map/ppermute | solution.py:14
  90.7 38.2 %collective-permute-start.8 = (bf16[1024,384]{0,1:T(8,128)(2,1)S(1)}, bf16[1024,384]{0,1:T(8,128)(2,1)S(1)}, u32[]{:S(2)}, u32[]{:S(2)}) collective-permute-start(bf16[1024,384]{0,1:T(8,128)(2,1)S(1)} %fusion), channel_id=1, source_target_pairs={{0,2},{1,3},{2,4},{3,5},{4,6},{5,7},{6,8},{7,9},{8,10},{9,11},{10,... | collective-permute-start | bytes 2359304 | tf_op jit(solution)/shard_map/ppermute | solution.py:14
  95.2 33.8 %collective-permute-start.7 = (bf16[1024,384]{0,1:T(8,128)(2,1)S(1)}, bf16[1024,384]{0,1:T(8,128)(2,1)S(1)}, u32[]{:S(2)}, u32[]{:S(2)}) collective-permute-start(bf16[1024,384]{0,1:T(8,128)(2,1)S(1)} %fusion), channel_id=1, source_target_pairs={{2,0},{3,1},{4,2},{5,3},{6,4},{7,5},{8,6},{9,7},{10,8},{11,9},{12,... | collective-permute-start | bytes 2359304 | tf_op jit(solution)/shard_map/ppermute | solution.py:14
  99.5 29.7 %copy-start.7 = (f32[1024,384]{0,1:T(8,128)S(1)}, f32[1024,384]{0,1:T(8,128)}, u32[]{:S(2)}) copy-start(f32[1024,384]{0,1:T(8,128)} %get-tuple-element.7) | copy-start | bytes 4718596
  129.2 3.1 %copy-start.5 = (bf16[1024,1152]{1,0:T(8,128)(2,1)S(1)}, bf16[1024,1152]{1,0:T(8,128)(2,1)}, u32[]{:S(2)}) copy-start(bf16[1024,1152]{1,0:T(8,128)(2,1)} %copy-done.4) | copy-start | bytes 7077892
  135.7 92.7 %all-reduce.2.cloned.1.call-start = ((), (), s32[]{:S(2)}) async-start(), calls=%async_computation.2 | async-start | bytes 1769472 | tf_op jit(solution)/shard_map/psum | solution.py:95
  135.8 41.9 %collective-permute-start.10 = (bf16[1024,384]{0,1:T(8,128)(2,1)S(1)}, bf16[1024,384]{0,1:T(8,128)(2,1)S(1)}, u32[]{:S(2)}, u32[]{:S(2)}) collective-permute-start(bf16[1024,384]{0,1:T(8,128)(2,1)S(1)} %get-tuple-element.8), channel_id=1, source_target_pairs={{0,1},{1,2},{2,3},{3,4},{4,5},{5,6},{6,7},{7,8},{8,9},{9,10},{10,1... | collective-permute-start | bytes 2359304 | tf_op jit(solution)/shard_map/ppermute | solution.py:14
  137.1 40.6 %collective-permute-start.9 = (bf16[1024,384]{0,1:T(8,128)(2,1)S(1)}, bf16[1024,384]{0,1:T(8,128)(2,1)S(1)}, u32[]{:S(2)}, u32[]{:S(2)}) collective-permute-start(bf16[1024,384]{0,1:T(8,128)(2,1)S(1)} %get-tuple-element.8), channel_id=1, source_target_pairs={{1,0},{2,1},{3,2},{4,3},{5,4},{6,5},{7,6},{8,7},{9,8},{10,9},{11,1... | collective-permute-start | bytes 2359304 | tf_op jit(solution)/shard_map/ppermute | solution.py:14
  177.6 1.4 copy-start.6
Sparse Core Ops, SparseCore 0:
  135.8 41.7 reduce-scatter.1
  180.1 48.2 all-reduce.1
